TPU v7x, 32 devices: a whole 2x2x4 slice. The times are simulated.
32 devices in a mesh: fsdp: 8 (over y, x, core), sp: 4 (over z).
Axes of the slice: x: 2, y: 2, z: 4, core: 2. Of those that a mesh axis runs over, the one named last changes fastest.
Arguments:
- hidden_in: bfloat16 [8, 1024, 2048], P('fsdp', 'sp'), may hold values from -6 to 6
- segments: int32 [8, 1024], P('fsdp'), may hold values from 0 to 3, never falling along the last dimension, each value on 1 to 640 neighbouring positions
- ln1_gain: float32 [2048], replicated, may hold values from 0.5 to 1.5
- ln1_bias: float32 [2048], replicated, may hold values from -1 to 1
- ln2_gain: float32 [2048], replicated, may hold values from 0.5 to 1.5
- ln2_bias: float32 [2048], replicated, may hold values from -1 to 1
- w_qkv: bfloat16 [6144, 2048], P('fsdp'), may hold values from -0.125 to 0.125
- b_qkv: float32 [6144], replicated, may hold values from -1 to 1
- w_dense: bfloat16 [2048, 2048], P('fsdp'), may hold values from -0.75 to 0.75
- b_dense: float32 [2048], replicated, may hold values from -1 to 1
- w_up: bfloat16 [8192, 2048], P('fsdp'), may hold values from -0.125 to 0.125
- b_up: float32 [8192], replicated, may hold values from -1 to 1
- w_down: bfloat16 [8192, 2048], P('fsdp'), may hold values from -0.0625 to 0.0625
- b_down: float32 [2048], replicated, may hold values from -1 to 1
- cotangent: bfloat16 [8, 1024, 2048], P('fsdp', 'sp'), may hold values from -6 to 6
Outputs:
- output: bfloat16 [8, 1024, 2048], P('fsdp', 'sp')
- input_grad: bfloat16 [8, 1024, 2048], P('fsdp', 'sp')
- grad_ln1_gain: float32 [2048], P('fsdp')
- grad_ln1_bias: float32 [2048], P('fsdp')
- grad_ln2_gain: float32 [2048], P('fsdp')
- grad_ln2_bias: float32 [2048], P('fsdp')
- grad_w_qkv: float32 [6144, 2048], P('fsdp')
- grad_b_qkv: float32 [6144], P('fsdp')
- grad_w_dense: float32 [2048, 2048], P('fsdp')
- grad_b_dense: float32 [2048], P('fsdp')
- grad_w_up: float32 [8192, 2048], P('fsdp')
- grad_b_up: float32 [8192], P('fsdp')
- grad_w_down: float32 [8192, 2048], P('fsdp')
- grad_b_down: float32 [2048], P('fsdp')
Inputs may be any that keep to these rules, and one draw needn't show every extreme that they name: `segments`: along each sequence the segment numbers never fall; each document is one run of 1 to 640 positions, and some document has exactly 640.
All inputs are finite; a program needn't handle non-finite values.
Results may differ from a plain program's by a relative error of at most 0.011.
Values may be sent and summed in bfloat16 or wider, within the bound.
A program may use at most 704 MiB of HBM per device.

v0:
```python
import math
import jax
import jax.numpy as jnp
from jax import lax
from jax.sharding import PartitionSpec as P

HEADS = 8
HEAD_DIM = 256
ROT = 64
EPSILON = 1e-05
NEGATIVE = -1e30
ROOT_HALF = 0.7071067811865476
ROOT_TWO_PI = 2.5066282746310002
SCALE = 1.0 / math.sqrt(HEAD_DIM)


def rounded(array):
    return lax.reduce_precision(array.astype(jnp.float32), 8, 7).astype(jnp.bfloat16)


def contract_rows(former, latter):
    return lax.dot_general(
        former, latter, (((0,), (0,)), ((), ())), preferred_element_type=jnp.float32
    )


def times_transposed(former, latter):
    return lax.dot_general(
        former, latter, (((1,), (1,)), ((), ())), preferred_element_type=jnp.float32
    )


def times(former, latter):
    return jnp.dot(former, latter, preferred_element_type=jnp.float32)


def norm_scaled(inputs):
    average = jnp.mean(inputs, axis=-1, keepdims=True)
    centred = inputs - average
    variance = jnp.mean(centred * centred, axis=-1, keepdims=True)
    inverse = lax.rsqrt(variance + EPSILON)
    return (centred * inverse, inverse)


def gelu_pair(hidden):
    cumulative = 0.5 * (1.0 + jax.scipy.special.erf(hidden * ROOT_HALF))
    return (
        hidden * cumulative,
        cumulative + hidden * jnp.exp(-0.5 * hidden * hidden) / ROOT_TWO_PI,
    )


def rotary_tables(segment_rows):
    length = segment_rows.shape[-1]
    places = jnp.arange(length, dtype=jnp.int32)
    changes = jnp.concatenate(
        [
            jnp.ones_like(segment_rows[..., :1]),
            (segment_rows[..., 1:] != segment_rows[..., :-1]).astype(jnp.int32),
        ],
        axis=-1,
    )
    first_place = lax.cummax(changes * places, axis=segment_rows.ndim - 1)
    position = (places - first_place).astype(jnp.float32)
    exponent = jnp.arange(0, ROT, 2).astype(jnp.float32) / ROT
    frequency = 1.0 / jnp.power(10000.0, exponent)
    angles = position[..., None] * frequency
    angles = jnp.concatenate([angles, angles], axis=-1)
    return (jnp.cos(angles), jnp.sin(angles))


def rotate(heads_part, cos_table, sin_table):
    half_rot = ROT // 2
    turned = heads_part[..., :ROT]
    swapped = jnp.concatenate([-turned[..., half_rot:], turned[..., :half_rot]], axis=-1)
    turned = turned * cos_table[..., None, :] + swapped * sin_table[..., None, :]
    return jnp.concatenate([turned, heads_part[..., ROT:]], axis=-1)


def unrotate(grads_part, cos_table, sin_table):
    half_rot = ROT // 2
    turned = grads_part[..., :ROT]
    along_sin = turned * sin_table[..., None, :]
    back_turn = jnp.concatenate([along_sin[..., half_rot:], -along_sin[..., :half_rot]], axis=-1)
    turned = turned * cos_table[..., None, :] + back_turn
    return jnp.concatenate([turned, grads_part[..., ROT:]], axis=-1)


def build_mask(segment_rows):
    places = jnp.arange(segment_rows.shape[-1], dtype=jnp.int32)
    return (segment_rows[:, :, None] == segment_rows[:, None, :]) & (
        places[None, :] <= places[:, None]
    )


def attention_scores(queries, keys_rot):
    return (
        jnp.einsum("bqhd,bkhd->bhqk", queries, keys_rot, preferred_element_type=jnp.float32) * SCALE
    )


def attend_forward(queries, keys_rot, values, mask):
    scores = jnp.where(mask[:, None], attention_scores(queries, keys_rot), NEGATIVE)
    row_top = jnp.max(scores, axis=-1, keepdims=True)
    exponent = jnp.exp(scores - row_top)
    row_total = jnp.sum(exponent, axis=-1, keepdims=True)
    attention = (exponent / row_total).astype(jnp.bfloat16)
    context = jnp.einsum("bhqk,bkhd->bqhd", attention, values, preferred_element_type=jnp.float32)
    return (context.astype(jnp.bfloat16), row_top + jnp.log(row_total))


def attend_backward(queries, keys_rot, values, mask, log_total, context_grad):
    scores = attention_scores(queries, keys_rot)
    attention = jnp.where(mask[:, None], jnp.exp(scores - log_total), 0.0)
    value_grad = jnp.einsum(
        "bhqk,bqhd->bkhd",
        attention.astype(jnp.bfloat16),
        context_grad,
        preferred_element_type=jnp.float32,
    )
    attention_grad = jnp.einsum(
        "bqhd,bkhd->bhqk", context_grad, values, preferred_element_type=jnp.float32
    )
    row_centre = jnp.sum(attention * attention_grad, axis=-1, keepdims=True)
    score_grad = (attention * (attention_grad - row_centre)).astype(jnp.bfloat16)
    query_grad = (
        jnp.einsum("bhqk,bkhd->bqhd", score_grad, keys_rot, preferred_element_type=jnp.float32)
        * SCALE
    )
    key_grad = (
        jnp.einsum("bhqk,bqhd->bkhd", score_grad, queries, preferred_element_type=jnp.float32)
        * SCALE
    )
    return (query_grad, key_grad, value_grad)


def sum_over_line(partial):
    inward = lax.ppermute(partial, "sp", [(0, 1), (3, 2)])
    half = rounded(partial.astype(jnp.float32) + inward.astype(jnp.float32))
    other = lax.ppermute(half, "sp", [(1, 2), (2, 1)])
    whole = rounded(half.astype(jnp.float32) + other.astype(jnp.float32))
    outward = lax.ppermute(whole, "sp", [(1, 0), (2, 3)])
    place = lax.axis_index("sp")
    inner = (place == 1) | (place == 2)
    return jnp.where(inner, whole, outward).astype(jnp.float32)


def sum_over_sp(partial):
    partial = rounded(partial)
    if lax.axis_size("sp") == 4:
        return sum_over_line(partial)
    return lax.psum(partial, "sp").astype(jnp.float32)


def per_device(
    hidden_in,
    segments,
    ln1_gain,
    ln1_bias,
    ln2_gain,
    ln2_bias,
    w_qkv,
    b_qkv,
    w_dense,
    b_dense,
    w_up,
    b_up,
    w_down,
    b_down,
    cotangent,
):
    seq_local, shard_len, width = hidden_in.shape
    seq_len = segments.shape[1]
    nf, ns = (lax.axis_size("fsdp"), lax.axis_size("sp"))
    f_place, s_place = (lax.axis_index("fsdp"), lax.axis_index("sp"))
    seqs = seq_local * nf
    group = seqs // ns
    piece = shard_len // nf
    tokens = group * seq_len
    per_head = max(1, nf // HEADS)
    head_count = max(1, HEADS // nf)
    head_sets = [[head * per_head + k for k in range(per_head)] for head in range(nf // per_head)]

    def gather_tokens(block):
        part = lax.all_to_all(block, "fsdp", split_axis=1, concat_axis=0, tiled=True)
        part = lax.all_to_all(part, "sp", split_axis=0, concat_axis=1, tiled=True)
        return lax.all_gather(part, "fsdp", axis=0, tiled=True).reshape(tokens, width)

    def scatter_tokens(partial):
        part = partial.reshape(nf * group, ns * piece, width)
        part = lax.psum_scatter(part, "fsdp", scatter_dimension=0, tiled=True)
        part = lax.all_to_all(part, "sp", split_axis=1, concat_axis=0, tiled=True)
        return lax.all_to_all(part, "fsdp", split_axis=0, concat_axis=1, tiled=True)

    def in_order(array):
        array = array.reshape(nf, group, ns, piece, -1)
        return array.transpose(1, 2, 0, 3, 4).reshape(group, seq_len, -1)

    def out_of_order(array):
        array = array.reshape(group, ns, nf, piece, -1)
        return array.transpose(2, 0, 1, 3, 4).reshape(tokens, -1)

    def over_head(array, axis):
        if per_head == 1:
            return array
        return lax.all_gather(array, "fsdp", axis=axis, tiled=True, axis_index_groups=head_sets)

    def own_columns(array):
        if per_head == 1:
            return array
        share = array.shape[-1] // per_head
        return lax.dynamic_slice_in_dim(array, f_place % per_head * share, share, array.ndim - 1)

    def own_part(vector):
        share = vector.shape[0] // nf
        return lax.dynamic_slice_in_dim(vector, f_place * share, share, 0)

    gathered = gather_tokens(hidden_in)
    upstream = gather_tokens(cotangent)
    rows = lax.all_gather(segments, "fsdp", axis=0, tiled=True)
    rows = lax.dynamic_slice_in_dim(rows, s_place * group, group, 0)
    dense_in = lax.all_to_all(w_dense, "fsdp", split_axis=1, concat_axis=0, tiled=True)
    head_qkv = over_head(w_qkv, 0)
    head_dense = over_head(dense_in, 1)
    head_bias = lax.dynamic_slice_in_dim(
        b_qkv, f_place // per_head * head_qkv.shape[0], head_qkv.shape[0], 0
    )
    scaled, _ = norm_scaled(gathered.astype(jnp.float32))
    normed = (scaled * ln1_gain + ln1_bias).astype(jnp.bfloat16)
    normed_mlp = (scaled * ln2_gain + ln2_bias).astype(jnp.bfloat16)
    hidden = times_transposed(normed_mlp, w_up) + own_part(b_up)
    activated, slope = gelu_pair(hidden)
    activated = activated.astype(jnp.bfloat16)
    hidden_grad = (times_transposed(upstream, w_down) * slope).astype(jnp.bfloat16)
    down_term = contract_rows(activated, upstream)
    up_term = contract_rows(hidden_grad, normed_mlp)
    mlp_norm_grad = times(hidden_grad, w_up)
    packed = (times_transposed(normed, head_qkv) + head_bias).astype(jnp.bfloat16)
    packed = in_order(packed).reshape(group, seq_len, head_count, 3 * HEAD_DIM)
    cos_table, sin_table = rotary_tables(rows)
    queries = rotate(packed[..., :HEAD_DIM].astype(jnp.float32), cos_table, sin_table).astype(
        jnp.bfloat16
    )
    keys_rot = rotate(
        packed[..., HEAD_DIM : 2 * HEAD_DIM].astype(jnp.float32), cos_table, sin_table
    ).astype(jnp.bfloat16)
    values = packed[..., 2 * HEAD_DIM :]
    mask = build_mask(rows)
    context, log_total = attend_forward(queries, keys_rot, values, mask)
    context = own_columns(out_of_order(context))
    partial_out = times_transposed(context, dense_in) + times(activated, w_down)
    context_grad = in_order(times(upstream, head_dense).astype(jnp.bfloat16)).reshape(
        group, seq_len, head_count, HEAD_DIM
    )
    query_grad, key_grad, value_grad = attend_backward(
        queries, keys_rot, values, mask, log_total, context_grad
    )
    packed_grad = jnp.concatenate(
        [
            unrotate(query_grad, cos_table, sin_table),
            unrotate(key_grad, cos_table, sin_table),
            value_grad,
        ],
        axis=-1,
    ).astype(jnp.bfloat16)
    packed_grad = own_columns(out_of_order(packed_grad))
    attn_norm_grad = times(packed_grad, w_qkv)
    qkv_term = contract_rows(packed_grad, normed)
    dense_term = contract_rows(upstream, context).astype(jnp.bfloat16)
    dense_term = lax.all_to_all(dense_term, "fsdp", split_axis=0, concat_axis=1, tiled=True)
    vectors = jnp.stack(
        [
            jnp.sum(attn_norm_grad * scaled, axis=0),
            jnp.sum(attn_norm_grad, axis=0),
            jnp.sum(mlp_norm_grad * scaled, axis=0),
            jnp.sum(mlp_norm_grad, axis=0),
        ],
        axis=1,
    )
    vectors = lax.psum_scatter(vectors, "fsdp", scatter_dimension=0, tiled=True)
    bias_out = own_part(jnp.sum(upstream.astype(jnp.float32), axis=0))
    bias_qkv = jnp.sum(packed_grad.astype(jnp.float32), axis=0)
    bias_up = jnp.sum(hidden_grad.astype(jnp.float32), axis=0)
    vectors, bias_out, bias_qkv, bias_up = lax.psum((vectors, bias_out, bias_qkv, bias_up), "sp")
    output = scatter_tokens(rounded(partial_out))
    weighted = scatter_tokens(rounded(attn_norm_grad * ln1_gain + mlp_norm_grad * ln2_gain))
    inputs = hidden_in.astype(jnp.float32)
    output = (inputs + (output.astype(jnp.float32) + (b_dense + b_down))).astype(jnp.bfloat16)
    own_scaled, own_inverse = norm_scaled(inputs)
    weighted = weighted.astype(jnp.float32)
    first_mean = jnp.mean(weighted, axis=-1, keepdims=True)
    second_mean = jnp.mean(weighted * own_scaled, axis=-1, keepdims=True)
    input_grad = (
        cotangent.astype(jnp.float32)
        + own_inverse * (weighted - first_mean - own_scaled * second_mean)
    ).astype(jnp.bfloat16)
    grad_down_w = sum_over_sp(down_term)
    grad_up_w = sum_over_sp(up_term)
    grad_qkv_w = sum_over_sp(qkv_term)
    grad_dense_w = sum_over_sp(dense_term)
    return (
        output,
        input_grad,
        vectors[:, 0],
        vectors[:, 1],
        vectors[:, 2],
        vectors[:, 3],
        grad_qkv_w,
        bias_qkv,
        grad_dense_w,
        bias_out,
        grad_up_w,
        bias_up,
        grad_down_w,
        bias_out,
    )


def solution(mesh):
    rows = P("fsdp", "sp", None)
    first = P("fsdp", None)
    return jax.shard_map(
        per_device,
        mesh=mesh,
        in_specs=(
            rows,
            first,
            P(),
            P(),
            P(),
            P(),
            first,
            P(),
            first,
            P(),
            first,
            P(),
            first,
            P(),
            rows,
        ),
        out_specs=(
            rows,
            rows,
            P("fsdp"),
            P("fsdp"),
            P("fsdp"),
            P("fsdp"),
            first,
            P("fsdp"),
            first,
            P("fsdp"),
            first,
            P("fsdp"),
            first,
            P("fsdp"),
        ),
        check_vma=False,
    )
```

profile of v0, /device:TPU:0, one launch (start us, length us, event | category | flops | bytes accessed | tf_op | source)
XLA Modules:
  0.0 1062.1 jit_solution(14219116837195556078)
XLA Ops:
  12.1 9.0 reduce.19
  23.7 20.6 %all_to_all.146 = bf16[8,2,32768]{2,1,0:T(2,128)(2,1)} all-to-all(bf16[8,2,32768]{2,1,0:T(2,128)(2,1)} %reshape.579), channel_id=1, replica_groups=mesh['fsdp'=8,'sp'=4] {'fsdp'}, dimensions={0} | all-to-all | bytes 2097152 | tf_op jit(solution)/shard_map/all_to_all | solution.py:185
  52.3 30.2 %all_to_all.147 = bf16[8,32,2048]{2,1,0:T(8,128)(2,1)S(1)} all-to-all(bf16[8,32,2048]{2,1,0:T(8,128)(2,1)S(1)} %bitcast.199), channel_id=1, replica_groups=mesh['fsdp'=8,'sp'=4] {'sp'}, dimensions={0} | all-to-all | bytes 2097152 | tf_op jit(solution)/shard_map/all_to_all | solution.py:186
  88.0 9.2 reduce.20
  99.8 26.8 %all_to_all.148 = bf16[8,2,32768]{2,1,0:T(2,128)(2,1)} all-to-all(bf16[8,2,32768]{2,1,0:T(2,128)(2,1)} %reshape.581), channel_id=1, replica_groups=mesh['fsdp'=8,'sp'=4] {'fsdp'}, dimensions={0} | all-to-all | bytes 2097152 | tf_op jit(solution)/shard_map/all_to_all | solution.py:185
  134.6 26.5 %all_to_all.149 = bf16[8,32,2048]{2,1,0:T(8,128)(2,1)S(1)} all-to-all(bf16[8,32,2048]{2,1,0:T(8,128)(2,1)S(1)} %bitcast.200), channel_id=1, replica_groups=mesh['fsdp'=8,'sp'=4] {'sp'}, dimensions={0} | all-to-all | bytes 2097152 | tf_op jit(solution)/shard_map/all_to_all | solution.py:186
  168.7 26.7 %all-gather = s32[8,1,1024]{2,1,0:T(1,128)S(1)} all-gather(s32[1,1,1024]{2,1,0:T(1,128)S(1)} %bitcast.233), channel_id=1, replica_groups=mesh['fsdp'=8,'sp'=4] {'fsdp'}, dimensions={0}, use_global_device_ids=true | all-gather | bytes 36864 | tf_op jit(solution)/shard_map/all_gather | solution.py:220
  212.1 7.4 add_convert_fusion.2
  219.4 7.1 add_convert_fusion.3
  287.8 7.0 concatenate.117
  298.7 15.7 %multiply_convert_fusion.1 = (bf16[2048,1024]{1,0:T(8,128)(2,1)}, f32[2048,1024]{1,0:T(8,128)}) fusion(f32[1024]{0:T(1024)S(1)} %dynamic_slice.14, bf16[2048,2048]{1,0:T(8,128)(2,1)} %get-tuple-element.26, bf16[1024,2048]{1,0:T(8,128)(2,1)S(1)} %copy-done.39), kind=kOutput, calls=%fused_computation.29 | convolution fusion | flops 8602517504 | bytes 25169920 | tf_op jit(solution)/shard_map/dot_general | solution.py:28
  314.4 17.5 %convert_reduce_fusion.2 = (f32[1024]{0:T(1024)}, bf16[2048,1024]{1,0:T(8,128)(2,1)}) fusion(f32[2048,1024]{1,0:T(8,128)} %get-tuple-element.60, f32[1024]{0:T(1024)S(1)} %dynamic_slice.14, bf16[2048,2048]{1,0:T(8,128)(2,1)S(1)} %bitcast.176, bf16[1024,2048]{1,0:T(8,128)(2,1)} %param.27), kind=kOutput, calls=%fused_computation.22 | convolution fusion | flops 8617196544 | bytes 25174016 | tf_op jit(solution)/shard_map/dot_general | solution.py:28
  331.9 14.1 %fusion.59 = f32[2048,2048]{1,0:T(8,128)} fusion(bf16[2048,1024]{1,0:T(8,128)(2,1)} %get-tuple-element.62, bf16[1024,2048]{1,0:T(8,128)(2,1)S(1)} %copy-done.39), kind=kOutput, calls=%fused_computation.148 | convolution fusion | flops 8589934592 | bytes 25165824 | tf_op jit(solution)/shard_map/dot_general | solution.py:34
  346.0 17.8 %multiply_reduce_fusion.1 = (f32[2048]{0:T(1024)S(1)}, f32[2048]{0:T(1024)S(1)}, f32[2048]{0:T(1024)S(1)}, f32[2048]{0:T(1024)S(1)}, bf16[2048,2048]{1,0:T(8,128)(2,1)}) fusion(bf16[16,128,2048]{2,1,0:T(8,128)(2,1)} %all-gather.4.cloned.1.call-done, f32[2048]{0:T(1024)S(1)} %get-tuple-element.48, f32[2048]{0:T(1024)S(1)} %get-tuple-element.49, ...), kind=kOutput, calls=%fused_computation.5 | convolution fusion | flops 6501163008 | bytes 39911424 | tf_op jit(solution)/shard_map/dot_general | solution.py:34
  365.0 7.5 fusion.31
  373.6 15.8 %reduce-precision_convert_fusion.7 = bf16[1024,2048]{1,0:T(8,128)(2,1)} fusion(bf16[2048,1024]{1,0:T(8,128)(2,1)} %get-tuple-element.62, bf16[2048,2048]{1,0:T(8,128)(2,1)} %get-tuple-element.26), kind=kOutput, calls=%fused_computation.25 | convolution fusion | flops 8594128896 | bytes 16777216 | tf_op jit(solution)/shard_map/dot_general | solution.py:22
  395.1 11.7 %fusion.58 = f32[2048,2048]{1,0:T(8,128)} fusion(bf16[2048,1024]{1,0:T(8,128)(2,1)S(1)} %copy-done.41, bf16[1024,2048]{1,0:T(8,128)(2,1)S(1)} %copy-done.40), kind=kOutput, calls=%fused_computation.147 | convolution fusion | flops 8589934592 | bytes 25165824 | tf_op jit(solution)/shard_map/dot_general | solution.py:34
  406.8 11.7 %reduce-precision_convert_fusion.1 = bf16[2048,2048]{1,0:T(8,128)(2,1)} fusion(f32[2048,2048]{1,0:T(8,128)} %fusion.58, bf16[2048,256]{1,0:T(8,128)(2,1)S(1)} %bitcast.188, bf16[2048,256]{1,0:T(8,128)(2,1)S(1)} %bitcast.212), kind=kOutput, calls=%fused_computation.7 | convolution fusion | flops 2160066560 | bytes 27262976 | tf_op jit(solution)/shard_map/dot_general | solution.py:28
  418.5 14.7 %reduce-precision_convert_fusion.4 = bf16[1024,2048]{1,0:T(8,128)(2,1)} fusion(bf16[2048,1024]{1,0:T(8,128)(2,1)} %get-tuple-element.59, bf16[2048,2048]{1,0:T(8,128)(2,1)} %bitcast.173), kind=kOutput, calls=%fused_computation.21 | convolution fusion | flops 8594128896 | bytes 16777216 | tf_op jit(solution)/shard_map/dot_general | solution.py:22
  436.5 6.3 add_convert_fusion
  442.8 8.3 reduce-precision_convert_fusion.10
  454.0 30.2 %collective-permute-done.6 = bf16[1024,2048]{1,0:T(8,128)(2,1)} collective-permute-done((bf16[1024,2048]{1,0:T(8,128)(2,1)}, bf16[1024,2048]{1,0:T(8,128)(2,1)}, u32[]{:S(2)}, u32[]{:S(2)}) %collective-permute-start.6) | collective-permute-done | bytes 4194336 | tf_op jit(solution)/shard_map/ppermute | solution.py:138
  484.3 7.9 reduce-precision_convert_fusion.6
  501.8 72.4 %collective-permute-done.9 = bf16[1024,2048]{1,0:T(8,128)(2,1)} collective-permute-done((bf16[1024,2048]{1,0:T(8,128)(2,1)}, bf16[1024,2048]{1,0:T(8,128)(2,1)}, u32[]{:S(2)}, u32[]{:S(2)}) %collective-permute-start.9) | collective-permute-done | bytes 4194336 | tf_op jit(solution)/shard_map/ppermute | solution.py:138
  574.1 7.7 reduce-precision_convert_fusion.3
  584.6 56.3 %collective-permute-done = bf16[768,2048]{1,0:T(8,128)(2,1)} collective-permute-done((bf16[768,2048]{1,0:T(8,128)(2,1)}, bf16[768,2048]{1,0:T(8,128)(2,1)}, u32[]{:S(2)}, u32[]{:S(2)}) %collective-permute-start) | collective-permute-done | bytes 3145760 | tf_op jit(solution)/shard_map/ppermute | solution.py:138
  655.6 20.9 %collective-permute-done.3 = bf16[256,2048]{1,0:T(8,128)(2,1)S(1)} collective-permute-done((bf16[256,2048]{1,0:T(8,128)(2,1)S(1)}, bf16[256,2048]{1,0:T(8,128)(2,1)S(1)}, u32[]{:S(2)}, u32[]{:S(2)}) %collective-permute-start.3) | collective-permute-done | bytes 1048608 | tf_op jit(solution)/shard_map/ppermute | solution.py:138
  677.6 7.7 reduce-precision_convert_fusion.5
  697.3 63.8 %all-to-all-start.7 = ((bf16[2,128,2048]{2,0,1:T(2,128)(2,1)}), bf16[2,128,2048]{2,0,1:T(2,128)(2,1)}, u32[]{:S(2)}, u32[]{:S(2)}) async-start(bf16[2,128,2048]{2,0,1:T(2,128)(2,1)} %copy.202), calls=%async_computation.9 | async-start | bytes 2097152 | tf_op jit(solution)/shard_map/all_to_all | solution.py:192
  761.2 7.7 reduce-precision_convert_fusion.2
  777.8 89.9 %all-to-all-done.7 = bf16[2,128,2048]{2,0,1:T(2,128)(2,1)} async-done(((bf16[2,128,2048]{2,0,1:T(2,128)(2,1)}), bf16[2,128,2048]{2,0,1:T(2,128)(2,1)}, u32[]{:S(2)}, u32[]{:S(2)}) %all-to-all-start.7) | async-done | bytes 1048608 | tf_op jit(solution)/shard_map/all_to_all | solution.py:192
  878.6 126.6 %all-reduce.1 = (f32[256,4]{0,1:T(4,128)S(1)}, f32[768]{0:T(1024)}, f32[256]{0:T(256)S(1)}, f32[1024]{0:T(1024)}) all-reduce(f32[256,4]{0,1:T(4,128)S(1)} %copy.219, f32[768]{0:T(1024)S(1)} %convert_reduce_fusion.3, f32[256]{0:T(256)S(1)} %dynamic_slice.15, f32[1024]{0:T(1024)S(1)} %copy-done.37), channel_id=1, replica_groups=mesh['fsdp'=8,'sp'=4] {'sp'}, use_global_device_ids=true, to_apply=%region_18.19 | all-reduce | flops 3072 | bytes 24576 | tf_op jit(solution)/shard_map/psum | solution.py:284
  (234 shorter events, 244.4 us)
Async XLA Ops:
  7.2 212.3 %copy-start = (bf16[768,2048]{1,0:T(8,128)(2,1)S(1)}, bf16[768,2048]{1,0:T(8,128)(2,1)}, u32[]{:S(2)}) copy-start(bf16[768,2048]{1,0:T(8,128)(2,1)} %param.21) | copy-start | bytes 9437188
  7.2 195.9 %all-gather.4.cloned.1.call-start = ((), (), s32[]{:S(2)}) async-start(), calls=%async_computation.13 | async-start | bytes 9437184 | tf_op jit(solution)/shard_map/all_gather | solution.py:187
  83.5 147.9 %all-gather.6.cloned.1.call-start = ((), (), s32[]{:S(2)}) async-start(), calls=%async_computation.15 | async-start | bytes 9437184 | tf_op jit(solution)/shard_map/all_gather | solution.py:187
  132.3 36.4 %copy-start.36 = (s32[1,1024]{1,0:T(1,128)S(1)}, s32[1,1024]{1,0:T(1,128)}, u32[]{:S(2)}) copy-start(s32[1,1024]{1,0:T(1,128)} %param.16) | copy-start | bytes 12292
  164.4 36.5 %all-to-all-start.2 = ((bf16[256,8,256]{0,2,1:T(8,128)(2,1)}), bf16[256,8,256]{0,2,1:T(8,128)(2,1)}, u32[]{:S(2)}, u32[]{:S(2)}) async-start(bf16[256,8,256]{0,2,1:T(8,128)(2,1)} %bitcast.204), calls=%async_computation.2 | async-start | bytes 2097152 | tf_op jit(solution)/shard_map/all_to_all | solution.py:222
  168.7 525.4 %reduce-scatter.8.cloned.1.call-start = ((), (), s32[]{:S(2)}) async-start(), calls=%async_computation.16 | async-start | bytes 9437184 | tf_op jit(solution)/shard_map/reduce_scatter | solution.py:191
  363.8 410.5 %reduce-scatter.6.cloned.1.call-start = ((), (), s32[]{:S(2)}) async-start(), calls=%async_computation.14 | async-start | bytes 9437184 | tf_op jit(solution)/shard_map/reduce_scatter | solution.py:191
  373.6 21.4 %copy-start.40 = (bf16[1024,2048]{1,0:T(8,128)(2,1)S(1)}, bf16[1024,2048]{1,0:T(8,128)(2,1)}, u32[]{:S(2)}) copy-start(bf16[1024,2048]{1,0:T(8,128)(2,1)} %param.27) | copy-start | bytes 12582916
  373.6 21.4 %copy-start.41 = (bf16[2048,1024]{1,0:T(8,128)(2,1)S(1)}, bf16[2048,1024]{1,0:T(8,128)(2,1)}, u32[]{:S(2)}) copy-start(bf16[2048,1024]{1,0:T(8,128)(2,1)} %get-tuple-element.59) | copy-start | bytes 12582916
  389.4 94.8 %collective-permute-start.6 = (bf16[1024,2048]{1,0:T(8,128)(2,1)}, bf16[1024,2048]{1,0:T(8,128)(2,1)}, u32[]{:S(2)}, u32[]{:S(2)}) collective-permute-start(bf16[1024,2048]{1,0:T(8,128)(2,1)} %reduce-precision_convert_fusion.7), channel_id=1, source_target_pairs={{0,1},{3,2},{4,5},{7,6},{8,9},{11,10},{12,13},{15,14},{16,17},{19,... | collective-permute-start | bytes 12582920 | tf_op jit(solution)/shard_map/ppermute | solution.py:138
  433.2 140.9 %collective-permute-start.9 = (bf16[1024,2048]{1,0:T(8,128)(2,1)}, bf16[1024,2048]{1,0:T(8,128)(2,1)}, u32[]{:S(2)}, u32[]{:S(2)}) collective-permute-start(bf16[1024,2048]{1,0:T(8,128)(2,1)} %reduce-precision_convert_fusion.4), channel_id=1, source_target_pairs={{0,1},{3,2},{4,5},{7,6},{8,9},{11,10},{12,13},{15,14},{16,17},{19,... | collective-permute-start | bytes 12582920 | tf_op jit(solution)/shard_map/ppermute | solution.py:138
  442.7 52.1 %slice-start.2 = ((s8[8388608]{0:T(1024)(128)(4,1)}), s8[4194304]{0:T(1024)(128)(4,1)S(1)}, s32[]{:S(2)}) async-start(s8[8388608]{0:T(1024)(128)(4,1)} %bitcast.177), calls=%async_computation.20 | async-start | bytes 8388608
  442.8 52.1 %slice-start.3 = ((s8[8388608]{0:T(1024)(128)(4,1)}), s8[4194304]{0:T(1024)(128)(4,1)S(1)}, s32[]{:S(2)}) async-start(s8[8388608]{0:T(1024)(128)(4,1)} %bitcast.177), calls=%async_computation.21 | async-start | bytes 8388608
  451.1 189.8 %collective-permute-start = (bf16[768,2048]{1,0:T(8,128)(2,1)}, bf16[768,2048]{1,0:T(8,128)(2,1)}, u32[]{:S(2)}, u32[]{:S(2)}) collective-permute-start(bf16[768,2048]{1,0:T(8,128)(2,1)} %reduce-precision_convert_fusion.10), channel_id=1, source_target_pairs={{0,1},{3,2},{4,5},{7,6},{8,9},{11,10},{12,13},{15,14},{16,17},{19,... | collective-permute-start | bytes 9437192 | tf_op jit(solution)/shard_map/ppermute | solution.py:138
  492.1 185.5 %collective-permute-start.7 = (bf16[1024,2048]{1,0:T(8,128)(2,1)}, bf16[1024,2048]{1,0:T(8,128)(2,1)}, u32[]{:S(2)}, u32[]{:S(2)}) collective-permute-start(bf16[1024,2048]{1,0:T(8,128)(2,1)} %reduce-precision_convert_fusion.6), channel_id=1, source_target_pairs={{1,2},{2,1},{5,6},{6,5},{9,10},{10,9},{13,14},{14,13},{17,18},{18,... | collective-permute-start | bytes 12582920 | tf_op jit(solution)/shard_map/ppermute | solution.py:140
  498.2 151.1 %all-to-all-start.9 = ((bf16[8,256,256]{1,2,0:T(8,128)(2,1)}), bf16[8,256,256]{1,2,0:T(8,128)(2,1)S(1)}, u32[]{:S(2)}, u32[]{:S(2)}) async-start(bf16[8,256,256]{1,2,0:T(8,128)(2,1)} %bitcast.164), calls=%async_computation.11 | async-start | bytes 2097152 | tf_op jit(solution)/shard_map/all_to_all | solution.py:270
  581.8 73.1 %copy-start.5 = (bf16[1,256,2048]{2,1,0:T(8,128)(2,1)S(1)}, bf16[1,256,2048]{2,1,0:T(8,128)(2,1)}, u32[]{:S(2)}) copy-start(bf16[1,256,2048]{2,1,0:T(8,128)(2,1)} %param.15) | copy-start | bytes 3145732
  581.8 179.4 %collective-permute-start.10 = (bf16[1024,2048]{1,0:T(8,128)(2,1)}, bf16[1024,2048]{1,0:T(8,128)(2,1)}, u32[]{:S(2)}, u32[]{:S(2)}) collective-permute-start(bf16[1024,2048]{1,0:T(8,128)(2,1)} %reduce-precision_convert_fusion.3), channel_id=1, source_target_pairs={{1,2},{2,1},{5,6},{6,5},{9,10},{10,9},{13,14},{14,13},{17,18},{18,... | collective-permute-start | bytes 12582920 | tf_op jit(solution)/shard_map/ppermute | solution.py:140
  647.0 39.6 %collective-permute-start.1 = (bf16[768,2048]{1,0:T(8,128)(2,1)}, bf16[768,2048]{1,0:T(8,128)(2,1)}, u32[]{:S(2)}, u32[]{:S(2)}) collective-permute-start(bf16[768,2048]{1,0:T(8,128)(2,1)} %reduce-precision_convert_fusion.9), channel_id=1, source_target_pairs={{1,2},{2,1},{5,6},{6,5},{9,10},{10,9},{13,14},{14,13},{17,18},{18,... | collective-permute-start | bytes 9437192 | tf_op jit(solution)/shard_map/ppermute | solution.py:140
  650.1 26.4 %collective-permute-start.3 = (bf16[256,2048]{1,0:T(8,128)(2,1)S(1)}, bf16[256,2048]{1,0:T(8,128)(2,1)S(1)}, u32[]{:S(2)}, u32[]{:S(2)}) collective-permute-start(bf16[256,2048]{1,0:T(8,128)(2,1)S(1)} %copy.206), channel_id=1, source_target_pairs={{0,1},{3,2},{4,5},{7,6},{8,9},{11,10},{12,13},{15,14},{16,17},{19,... | collective-permute-start | bytes 3145736 | tf_op jit(solution)/shard_map/ppermute | solution.py:138
  676.9 93.4 %collective-permute-start.4 = (bf16[256,2048]{1,0:T(8,128)(2,1)S(1)}, bf16[256,2048]{1,0:T(8,128)(2,1)S(1)}, u32[]{:S(2)}, u32[]{:S(2)}) collective-permute-start(bf16[256,2048]{1,0:T(8,128)(2,1)S(1)} %reduce-precision_convert_fusion.12), channel_id=1, source_target_pairs={{1,2},{2,1},{5,6},{6,5},{9,10},{10,9},{13,14},{14,13},{17,18},{18,... | collective-permute-start | bytes 3145736 | tf_op jit(solution)/shard_map/ppermute | solution.py:140
  685.3 334.4 %collective-permute-start.8 = (bf16[1024,2048]{1,0:T(8,128)(2,1)}, bf16[1024,2048]{1,0:T(8,128)(2,1)}, u32[]{:S(2)}, u32[]{:S(2)}) collective-permute-start(bf16[1024,2048]{1,0:T(8,128)(2,1)} %reduce-precision_convert_fusion.5), channel_id=1, source_target_pairs={{1,0},{2,3},{5,4},{6,7},{9,8},{10,11},{13,12},{14,15},{17,16},{18,... | collective-permute-start | bytes 12582920 | tf_op jit(solution)/shard_map/ppermute | solution.py:142
  692.7 322.0 %collective-permute-start.2 = (bf16[768,2048]{1,0:T(8,128)(2,1)}, bf16[768,2048]{1,0:T(8,128)(2,1)}, u32[]{:S(2)}, u32[]{:S(2)}) collective-permute-start(bf16[768,2048]{1,0:T(8,128)(2,1)} %reduce-precision_convert_fusion.8), channel_id=1, source_target_pairs={{1,0},{2,3},{5,4},{6,7},{9,8},{10,11},{13,12},{14,15},{17,16},{18,... | collective-permute-start | bytes 9437192 | tf_op jit(solution)/shard_map/ppermute | solution.py:142
  697.3 170.4 %all-to-all-start.7 = ((bf16[2,128,2048]{2,0,1:T(2,128)(2,1)}), bf16[2,128,2048]{2,0,1:T(2,128)(2,1)}, u32[]{:S(2)}, u32[]{:S(2)}) async-start(bf16[2,128,2048]{2,0,1:T(2,128)(2,1)} %copy.202), calls=%async_computation.9 | async-start | bytes 2097152 | tf_op jit(solution)/shard_map/all_to_all | solution.py:192
  761.1 116.5 %reduce-scatter.10.cloned.1.call-start = ((), (), s32[]{:S(2)}) async-start(), calls=%async_computation.17 | async-start | bytes 1179648
  768.9 265.4 %collective-permute-start.11 = (bf16[1024,2048]{1,0:T(8,128)(2,1)}, bf16[1024,2048]{1,0:T(8,128)(2,1)}, u32[]{:S(2)}, u32[]{:S(2)}) collective-permute-start(bf16[1024,2048]{1,0:T(8,128)(2,1)} %reduce-precision_convert_fusion.2), channel_id=1, source_target_pairs={{1,0},{2,3},{5,4},{6,7},{9,8},{10,11},{13,12},{14,15},{17,16},{18,... | collective-permute-start | bytes 12582920 | tf_op jit(solution)/shard_map/ppermute | solution.py:142
  771.6 234.2 %collective-permute-start.5 = (bf16[256,2048]{1,0:T(8,128)(2,1)}, bf16[256,2048]{1,0:T(8,128)(2,1)}, u32[]{:S(2)}, u32[]{:S(2)}) collective-permute-start(bf16[256,2048]{1,0:T(8,128)(2,1)} %reduce-precision_convert_fusion.11), channel_id=1, source_target_pairs={{1,0},{2,3},{5,4},{6,7},{9,8},{10,11},{13,12},{14,15},{17,16},{18,... | collective-permute-start | bytes 3145736 | tf_op jit(solution)/shard_map/ppermute | solution.py:142
  774.3 102.7 %copy-start.4 = (bf16[2,4,8,32,768]{4,3,2,1,0:T(8,128)(2,1)S(1)}, bf16[2,4,8,32,768]{4,3,2,1,0:T(8,128)(2,1)}, u32[]{:S(2)}) copy-start(bf16[2,4,8,32,768]{4,3,2,1,0:T(8,128)(2,1)} %concatenate.117) | copy-start | bytes 9437188
  867.7 143.4 %all-to-all-start.3 = ((bf16[2,128,2048]{2,0,1:T(2,128)(2,1)}), bf16[2,128,2048]{2,0,1:T(2,128)(2,1)}, u32[]{:S(2)}, u32[]{:S(2)}) async-start(bf16[2,128,2048]{2,0,1:T(2,128)(2,1)} %copy.186), calls=%async_computation.4 | async-start | bytes 2097152 | tf_op jit(solution)/shard_map/all_to_all | solution.py:192
  1005.2 49.4 %copy-start.38 = (f32[256]{0:T(256)}, f32[256]{0:T(256)S(1)}, u32[]{:S(2)}) copy-start(f32[256]{0:T(256)S(1)} %get-tuple-element.92) | copy-start | bytes 3076
  1011.2 18.9 %all-to-all-start.8 = ((bf16[8,32,2048]{2,1,0:T(8,128)(2,1)}), bf16[8,32,2048]{2,1,0:T(8,128)(2,1)S(1)}, u32[]{:S(2)}, u32[]{:S(2)}) async-start(bf16[8,32,2048]{2,1,0:T(8,128)(2,1)} %bitcast.55), calls=%async_computation.10 | async-start | bytes 2097152 | tf_op jit(solution)/shard_map/all_to_all | solution.py:193
  1030.1 19.7 %all-to-all-start.4 = ((bf16[8,32,2048]{2,1,0:T(8,128)(2,1)}), bf16[8,32,2048]{2,1,0:T(8,128)(2,1)}, u32[]{:S(2)}, u32[]{:S(2)}) async-start(bf16[8,32,2048]{2,1,0:T(8,128)(2,1)} %bitcast.27), calls=%async_computation.5 | async-start | bytes 2097152 | tf_op jit(solution)/shard_map/all_to_all | solution.py:193
  (37 other events, 272.3 us)
Sparse Core Ops, SparseCore 0:
  83.7 59.1 all-gather.3
  162.2 62.2 all-gather.5
  364.0 71.4 reduce-scatter.7
  439.7 78.5 reduce-scatter.5
  774.4 44.9 reduce-scatter.9
where the time goes:
time: 1070 us; the launch traced here: 1060 us
  waiting for transfers between devices  276 us (26%)
  blocking collectives  257 us (24%)
  matrix products  168 us (16%)
  other arithmetic  151 us (14%)
  starting transfers between devices  115 us (11%)
  local copies, waits for them, and re-layouts  79.8 us (7%)
  between operations  15.1 us (1%)
    ppermute x4, waiting for transfers between devices, sum_over_line(): inward = lax.ppermute(partial, 'sp', [(0, 1), (3, 2)])  180 us
    psum x1, blocking collectives, per_device(): lax.psum((vectors, bias_out, bias_qkv, bias_up), 'sp')  127 us
    all_to_all x2, waiting for transfers between devices, scatter_tokens(): part = lax.all_to_all(part, 'sp', split_axis=1, concat_axis=0, tiled=True)  89.9 us
    all_to_all x2, starting transfers between devices, scatter_tokens(): part = lax.all_to_all(part, 'sp', split_axis=1, concat_axis=0, tiled=True)  68.4 us
    all_to_all x2, blocking collectives, gather_tokens(): part = lax.all_to_all(part, 'sp', split_axis=0, concat_axis=1, tiled=True)  56.6 us
    dot_general x4, matrix products, times_transposed(): lax.dot_general(former, latter, (((1,), (1,)), ((), ())), preferred_eleme...  52 us
    dot_general x4, matrix products, times(): return jnp.dot(former, latter, preferred_element_type=jnp.float32)  49.7 us
    all_to_all x2, blocking collectives, gather_tokens(): lax.all_to_all(block, 'fsdp', split_axis=1, concat_axis=0, tiled=True)  47.4 us
  transfers between devices with their start and end apart: 23, of which 7 were waited for; matrix products, arithmetic and copies ran while one was open for 22% of the time, Pallas kernels for 0%

commit v1 on v0

--- a/solution.py
+++ b/solution.py
@@ -1,3 +1,4 @@
+import functools
 import math
 import jax
 import jax.numpy as jnp
@@ -12,6 +13,34 @@
 ROOT_HALF = 0.7071067811865476
 ROOT_TWO_PI = 2.5066282746310002
 SCALE = 1.0 / math.sqrt(HEAD_DIM)
+
+
+def groups_register(q_in, out_dim, own_rows):
+    small, z = (q_in.shape[:out_dim], q_in.shape[out_dim + 1 :])
+    current_block = jnp.moveaxis(q_in.reshape(*small, own_rows, -1, *z), out_dim, 0)
+    return current_block
+
+
+def process_members_all(local, which_dim):
+    high = list(local.shape[1:])
+    high[which_dim] *= local.shape[0]
+    frame_out = jnp.moveaxis(local, 0, which_dim).reshape(high)
+    return frame_out
+
+
+def cards_group(vals, lane_axis, incoming_x, field_in):
+    y, piece_out = (jax.lax.axis_size(lane_axis), jax.lax.axis_index(lane_axis))
+    front = groups_register(vals, incoming_x, y)
+    cards = [front[piece_out]]
+    for dev_j in range(1, y):
+        x_new = front[piece_out ^ dev_j]
+        cards.append(jax.lax.ppermute(x_new, lane_axis, [(it, it ^ dev_j) for it in range(y)]))
+    front = jnp.stack(cards)[piece_out ^ jnp.arange(y)]
+    reply = process_members_all(front, field_in)
+    return reply
+
+
+fill_works_on_mesh = functools.partial(cards_group, lane_axis="sp", incoming_x=0, field_in=1)
 
 
 def rounded(array):
@@ -183,7 +212,7 @@
 
     def gather_tokens(block):
         part = lax.all_to_all(block, "fsdp", split_axis=1, concat_axis=0, tiled=True)
-        part = lax.all_to_all(part, "sp", split_axis=0, concat_axis=1, tiled=True)
+        part = fill_works_on_mesh(part)
         return lax.all_gather(part, "fsdp", axis=0, tiled=True).reshape(tokens, width)
 
     def scatter_tokens(partial):

time: 1070 us -> 1070 us (level)
  blocking collectives: 257 us -> 176 us
  waiting for transfers between devices: 276 us -> 330 us
  starting transfers between devices: 115 us -> 126 us
    all_to_all x2 -> x0, blocking collectives: 56.6 us -> none  [gather_tokens(): part = lax.all_to_all(part, 'sp', split_axis=0, concat_axis=1, tiled=True)]
    ppermute x0 -> x6, waiting for transfers between devices: none -> 37.9 us  [cards_group(): jax.lax.ppermute(x_new, lane_axis, [(it, it ^ dev_j) for it in range(y)])]
    all_to_all x2 -> x1, blocking collectives: 47.4 us -> 20.7 us  [gather_tokens(): lax.all_to_all(block, 'fsdp', split_axis=1, concat_axis=0, tiled=True)]
    all_to_all x0 -> x1, waiting for transfers between devices: none -> 15.5 us  [gather_tokens(): lax.all_to_all(block, 'fsdp', split_axis=1, concat_axis=0, tiled=True)]
    convert_element_type x9 -> x8, other arithmetic: 45 us -> 44.9 us  [rounded(): lax.reduce_precision(array.astype(jnp.float32), 8, 7).astype(jnp.bfloat16)]
  transfers between devices with their start and end apart: 23 -> 30, of which waited for: 7 -> 12; matrix products, arithmetic and copies ran while one was open for 22% -> 23% of each run, Pallas kernels for 0% -> 0%
where the time goes in v1:
time: 1070 us; the launch traced here: 1060 us
  waiting for transfers between devices  330 us (31%)
  blocking collectives  176 us (16%)
  matrix products  170 us (16%)
  other arithmetic  153 us (14%)
  starting transfers between devices  126 us (12%)
  local copies, waits for them, and re-layouts  86.8 us (8%)
  between operations  15.1 us (1%)
    ppermute x4, waiting for transfers between devices, sum_over_line(): inward = lax.ppermute(partial, 'sp', [(0, 1), (3, 2)])  180 us
    psum x1, blocking collectives, per_device(): lax.psum((vectors, bias_out, bias_qkv, bias_up), 'sp')  127 us
    all_to_all x2, waiting for transfers between devices, scatter_tokens(): part = lax.all_to_all(part, 'sp', split_axis=1, concat_axis=0, tiled=True)  90.2 us
    all_to_all x2, starting transfers between devices, scatter_tokens(): part = lax.all_to_all(part, 'sp', split_axis=1, concat_axis=0, tiled=True)  68.4 us
    dot_general x4, matrix products, times_transposed(): lax.dot_general(former, latter, (((1,), (1,)), ((), ())), preferred_eleme...  51.9 us
    dot_general x4, matrix products, times(): return jnp.dot(former, latter, preferred_element_type=jnp.float32)  49.7 us
    convert_element_type x8, other arithmetic, rounded(): lax.reduce_precision(array.astype(jnp.float32), 8, 7).astype(jnp.bfloat16)  44.9 us
    dot_general x4, matrix products, contract_rows(): lax.dot_general(former, latter, (((0,), (0,)), ((), ())), preferred_eleme...  42.1 us
  transfers between devices with their start and end apart: 30, of which 12 were waited for; matrix products, arithmetic and copies ran while one was open for 23% of the time, Pallas kernels for 0%

profile of v1, /device:TPU:0, one launch (start us, length us, event | category | flops | bytes accessed | tf_op | source)
XLA Modules:
  0.0 1056.6 jit_solution(1930040438688394198)
XLA Ops:
  12.0 9.0 reduce.19
  28.9 15.5 %all-to-all-done = bf16[8,2,32768]{2,1,0:T(2,128)(2,1)} async-done(((bf16[8,2,32768]{2,1,0:T(2,128)(2,1)}), bf16[8,2,32768]{2,1,0:T(2,128)(2,1)}, u32[]{:S(2)}, u32[]{:S(2)}) %all-to-all-start) | async-done | bytes 1048608 | tf_op jit(solution)/shard_map/all_to_all | solution.py:214
  63.7 12.1 %collective-permute-done.1 = bf16[2,32,2048]{2,1,0:T(8,128)(2,1)S(1)} collective-permute-done((bf16[2,32,2048]{2,1,0:T(8,128)(2,1)S(1)}, bf16[2,32,2048]{2,1,0:T(8,128)(2,1)S(1)}, u32[]{:S(2)}, u32[]{:S(2)}) %collective-permute-start.1) | collective-permute-done | bytes 262176 | tf_op jit(solution)/shard_map/ppermute | solution.py:37
  86.5 9.0 reduce.20
  98.1 20.7 %all_to_all.104 = bf16[8,2,32768]{2,1,0:T(2,128)(2,1)} all-to-all(bf16[8,2,32768]{2,1,0:T(2,128)(2,1)} %reshape.631), channel_id=1, replica_groups=mesh['fsdp'=8,'sp'=4] {'fsdp'}, dimensions={0} | all-to-all | bytes 2097152 | tf_op jit(solution)/shard_map/all_to_all | solution.py:214
  131.4 6.8 collective-permute-done.5
  138.2 12.5 %collective-permute-done.4 = bf16[2,32,2048]{2,1,0:T(8,128)(2,1)S(1)} collective-permute-done((bf16[2,32,2048]{2,1,0:T(8,128)(2,1)S(1)}, bf16[2,32,2048]{2,1,0:T(8,128)(2,1)S(1)}, u32[]{:S(2)}, u32[]{:S(2)}) %collective-permute-start.4) | collective-permute-done | bytes 262176 | tf_op jit(solution)/shard_map/ppermute | solution.py:37
  163.5 28.1 %all-gather = s32[8,1,1024]{2,1,0:T(1,128)S(1)} all-gather(s32[1,1,1024]{2,1,0:T(1,128)S(1)} %bitcast.252), channel_id=1, replica_groups=mesh['fsdp'=8,'sp'=4] {'fsdp'}, dimensions={0}, use_global_device_ids=true | all-gather | bytes 36864 | tf_op jit(solution)/shard_map/all_gather | solution.py:249
  208.2 7.4 add_convert_fusion.2
  215.6 7.1 add_convert_fusion.3
  284.0 7.0 concatenate.117
  295.0 15.7 %multiply_convert_fusion.1 = (bf16[2048,1024]{1,0:T(8,128)(2,1)}, f32[2048,1024]{1,0:T(8,128)}) fusion(f32[1024]{0:T(1024)S(1)} %dynamic_slice.42, bf16[2048,2048]{1,0:T(8,128)(2,1)} %get-tuple-element.26, bf16[1024,2048]{1,0:T(8,128)(2,1)S(1)} %copy-done.39), kind=kOutput, calls=%fused_computation.31 | convolution fusion | flops 8602517504 | bytes 25169920 | tf_op jit(solution)/shard_map/dot_general | solution.py:57
  310.6 17.5 %convert_reduce_fusion.2 = (f32[1024]{0:T(1024)}, bf16[2048,1024]{1,0:T(8,128)(2,1)}) fusion(f32[2048,1024]{1,0:T(8,128)} %get-tuple-element.68, f32[1024]{0:T(1024)S(1)} %dynamic_slice.42, bf16[2048,2048]{1,0:T(8,128)(2,1)S(1)} %bitcast.197, bf16[1024,2048]{1,0:T(8,128)(2,1)} %param.27), kind=kOutput, calls=%fused_computation.24 | convolution fusion | flops 8617196544 | bytes 25174016 | tf_op jit(solution)/shard_map/dot_general | solution.py:57
  328.1 14.1 %fusion.61 = f32[2048,2048]{1,0:T(8,128)} fusion(bf16[2048,1024]{1,0:T(8,128)(2,1)} %get-tuple-element.70, bf16[1024,2048]{1,0:T(8,128)(2,1)S(1)} %copy-done.39), kind=kOutput, calls=%fused_computation.163 | convolution fusion | flops 8589934592 | bytes 25165824 | tf_op jit(solution)/shard_map/dot_general | solution.py:63
  342.2 17.8 %multiply_reduce_fusion.1 = (f32[2048]{0:T(1024)S(1)}, f32[2048]{0:T(1024)S(1)}, f32[2048]{0:T(1024)S(1)}, f32[2048]{0:T(1024)S(1)}, bf16[2048,2048]{1,0:T(8,128)(2,1)}) fusion(bf16[16,128,2048]{2,1,0:T(8,128)(2,1)} %all-gather.4.cloned.1.call-done, f32[2048]{0:T(1024)S(1)} %get-tuple-element.56, f32[2048]{0:T(1024)S(1)} %get-tuple-element.57, ...), kind=kOutput, calls=%fused_computation.7 | convolution fusion | flops 6501163008 | bytes 39911424 | tf_op jit(solution)/shard_map/dot_general | solution.py:63
  361.2 8.2 fusion.31
  370.5 15.4 %reduce-precision_convert_fusion.7 = bf16[1024,2048]{1,0:T(8,128)(2,1)} fusion(bf16[2048,1024]{1,0:T(8,128)(2,1)} %get-tuple-element.70, bf16[2048,2048]{1,0:T(8,128)(2,1)} %get-tuple-element.26), kind=kOutput, calls=%fused_computation.27 | convolution fusion | flops 8594128896 | bytes 16777216 | tf_op jit(solution)/shard_map/dot_general | solution.py:51
  389.2 11.7 %fusion.60 = f32[2048,2048]{1,0:T(8,128)} fusion(bf16[2048,1024]{1,0:T(8,128)(2,1)S(1)} %copy-done.41, bf16[1024,2048]{1,0:T(8,128)(2,1)S(1)} %copy-done.40), kind=kOutput, calls=%fused_computation.162 | convolution fusion | flops 8589934592 | bytes 25165824 | tf_op jit(solution)/shard_map/dot_general | solution.py:63
  400.9 11.7 %reduce-precision_convert_fusion.1 = bf16[2048,2048]{1,0:T(8,128)(2,1)} fusion(f32[2048,2048]{1,0:T(8,128)} %fusion.60, bf16[2048,256]{1,0:T(8,128)(2,1)S(1)} %bitcast.224, bf16[2048,256]{1,0:T(8,128)(2,1)S(1)} %bitcast.223), kind=kOutput, calls=%fused_computation.9 | convolution fusion | flops 2160066560 | bytes 27262976 | tf_op jit(solution)/shard_map/dot_general | solution.py:57
  412.7 14.7 %reduce-precision_convert_fusion.4 = bf16[1024,2048]{1,0:T(8,128)(2,1)} fusion(bf16[2048,1024]{1,0:T(8,128)(2,1)} %get-tuple-element.67, bf16[2048,2048]{1,0:T(8,128)(2,1)} %bitcast.194), kind=kOutput, calls=%fused_computation.23 | convolution fusion | flops 8594128896 | bytes 16777216 | tf_op jit(solution)/shard_map/dot_general | solution.py:51
  436.9 8.3 reduce-precision_convert_fusion.10
  448.3 30.1 %collective-permute-done.12 = bf16[1024,2048]{1,0:T(8,128)(2,1)} collective-permute-done((bf16[1024,2048]{1,0:T(8,128)(2,1)}, bf16[1024,2048]{1,0:T(8,128)(2,1)}, u32[]{:S(2)}, u32[]{:S(2)}) %collective-permute-start.12) | collective-permute-done | bytes 4194336 | tf_op jit(solution)/shard_map/ppermute | solution.py:167
  478.4 7.9 reduce-precision_convert_fusion.6
  496.2 72.1 %collective-permute-done.15 = bf16[1024,2048]{1,0:T(8,128)(2,1)} collective-permute-done((bf16[1024,2048]{1,0:T(8,128)(2,1)}, bf16[1024,2048]{1,0:T(8,128)(2,1)}, u32[]{:S(2)}, u32[]{:S(2)}) %collective-permute-start.15) | collective-permute-done | bytes 4194336 | tf_op jit(solution)/shard_map/ppermute | solution.py:167
  568.3 7.7 reduce-precision_convert_fusion.3
  578.8 56.5 %collective-permute-done.6 = bf16[768,2048]{1,0:T(8,128)(2,1)} collective-permute-done((bf16[768,2048]{1,0:T(8,128)(2,1)}, bf16[768,2048]{1,0:T(8,128)(2,1)}, u32[]{:S(2)}, u32[]{:S(2)}) %collective-permute-start.6) | collective-permute-done | bytes 3145760 | tf_op jit(solution)/shard_map/ppermute | solution.py:167
  648.9 21.5 %collective-permute-done.9 = bf16[256,2048]{1,0:T(8,128)(2,1)S(1)} collective-permute-done((bf16[256,2048]{1,0:T(8,128)(2,1)S(1)}, bf16[256,2048]{1,0:T(8,128)(2,1)S(1)}, u32[]{:S(2)}, u32[]{:S(2)}) %collective-permute-start.9) | collective-permute-done | bytes 1048608 | tf_op jit(solution)/shard_map/ppermute | solution.py:167
  671.6 7.7 reduce-precision_convert_fusion.5
  691.3 63.9 %all-to-all-start.5 = ((bf16[2,128,2048]{2,0,1:T(2,128)(2,1)}), bf16[2,128,2048]{2,0,1:T(2,128)(2,1)}, u32[]{:S(2)}, u32[]{:S(2)}) async-start(bf16[2,128,2048]{2,0,1:T(2,128)(2,1)} %copy.195), calls=%async_computation.7 | async-start | bytes 2097152 | tf_op jit(solution)/shard_map/all_to_all | solution.py:221
  755.3 7.7 reduce-precision_convert_fusion.2
  771.9 90.2 %all-to-all-done.5 = bf16[2,128,2048]{2,0,1:T(2,128)(2,1)} async-done(((bf16[2,128,2048]{2,0,1:T(2,128)(2,1)}), bf16[2,128,2048]{2,0,1:T(2,128)(2,1)}, u32[]{:S(2)}, u32[]{:S(2)}) %all-to-all-start.5) | async-done | bytes 1048608 | tf_op jit(solution)/shard_map/all_to_all | solution.py:221
  872.9 126.8 %all-reduce.1 = (f32[256,4]{0,1:T(4,128)S(1)}, f32[768]{0:T(1024)}, f32[256]{0:T(256)S(1)}, f32[1024]{0:T(1024)}) all-reduce(f32[256,4]{0,1:T(4,128)S(1)} %copy.210, f32[768]{0:T(1024)S(1)} %convert_reduce_fusion.3, f32[256]{0:T(256)S(1)} %dynamic_slice.47, f32[1024]{0:T(1024)S(1)} %copy-done.37), channel_id=1, replica_groups=mesh['fsdp'=8,'sp'=4] {'sp'}, use_global_device_ids=true, to_apply=%region_18.19 | all-reduce | flops 3072 | bytes 24576 | tf_op jit(solution)/shard_map/psum | solution.py:313
  (252 shorter events, 279.2 us)
Async XLA Ops:
  7.2 208.4 %copy-start = (bf16[768,2048]{1,0:T(8,128)(2,1)S(1)}, bf16[768,2048]{1,0:T(8,128)(2,1)}, u32[]{:S(2)}) copy-start(bf16[768,2048]{1,0:T(8,128)(2,1)} %param.21) | copy-start | bytes 9437188
  23.6 20.7 %all-to-all-start = ((bf16[8,2,32768]{2,1,0:T(2,128)(2,1)}), bf16[8,2,32768]{2,1,0:T(2,128)(2,1)}, u32[]{:S(2)}, u32[]{:S(2)}) async-start(bf16[8,2,32768]{2,1,0:T(2,128)(2,1)} %reshape.629), calls=%async_computation | async-start | bytes 2097152 | tf_op jit(solution)/shard_map/all_to_all | solution.py:214
  28.8 170.4 %all-gather.4.cloned.1.call-start = ((), (), s32[]{:S(2)}) async-start(), calls=%async_computation.11 | async-start | bytes 9437184 | tf_op jit(solution)/shard_map/all_gather | solution.py:216
  52.4 11.3 %collective-permute-start.2 = (bf16[2,32,2048]{2,1,0:T(8,128)(2,1)S(1)}, bf16[2,32,2048]{2,1,0:T(8,128)(2,1)S(1)}, u32[]{:S(2)}, u32[]{:S(2)}) collective-permute-start(bf16[2,32,2048]{2,1,0:T(8,128)(2,1)S(1)} %get-tuple-element.52), channel_id=1, source_target_pairs={{0,3},{1,2},{2,1},{3,0},{4,7},{5,6},{6,5},{7,4},{8,11},{9,10},{10,... | collective-permute-start | bytes 786440 | tf_op jit(solution)/shard_map/ppermute | solution.py:37
  56.5 19.3 %collective-permute-start.1 = (bf16[2,32,2048]{2,1,0:T(8,128)(2,1)S(1)}, bf16[2,32,2048]{2,1,0:T(8,128)(2,1)S(1)}, u32[]{:S(2)}, u32[]{:S(2)}) collective-permute-start(bf16[2,32,2048]{2,1,0:T(8,128)(2,1)S(1)} %get-tuple-element.53), channel_id=1, source_target_pairs={{0,2},{1,3},{2,0},{3,1},{4,6},{5,7},{6,4},{7,5},{8,10},{9,11},{10,... | collective-permute-start | bytes 786440 | tf_op jit(solution)/shard_map/ppermute | solution.py:37
  56.5 19.3 %collective-permute-start = (bf16[2,32,2048]{2,1,0:T(8,128)(2,1)S(1)}, bf16[2,32,2048]{2,1,0:T(8,128)(2,1)S(1)}, u32[]{:S(2)}, u32[]{:S(2)}) collective-permute-start(bf16[2,32,2048]{2,1,0:T(8,128)(2,1)S(1)} %get-tuple-element.54), channel_id=1, source_target_pairs={{0,1},{1,0},{2,3},{3,2},{4,5},{5,4},{6,7},{7,6},{8,9},{9,8},{10,11... | collective-permute-start | bytes 786440 | tf_op jit(solution)/shard_map/ppermute | solution.py:37
  82.1 145.6 %all-gather.6.cloned.1.call-start = ((), (), s32[]{:S(2)}) async-start(), calls=%async_computation.13 | async-start | bytes 9437184 | tf_op jit(solution)/shard_map/all_gather | solution.py:216
  127.0 11.2 %collective-permute-start.5 = (bf16[2,32,2048]{2,1,0:T(8,128)(2,1)S(1)}, bf16[2,32,2048]{2,1,0:T(8,128)(2,1)S(1)}, u32[]{:S(2)}, u32[]{:S(2)}) collective-permute-start(bf16[2,32,2048]{2,1,0:T(8,128)(2,1)S(1)} %get-tuple-element.46), channel_id=1, source_target_pairs={{0,3},{1,2},{2,1},{3,0},{4,7},{5,6},{6,5},{7,4},{8,11},{9,10},{10,... | collective-permute-start | bytes 786440 | tf_op jit(solution)/shard_map/ppermute | solution.py:37
  129.2 21.5 %collective-permute-start.4 = (bf16[2,32,2048]{2,1,0:T(8,128)(2,1)S(1)}, bf16[2,32,2048]{2,1,0:T(8,128)(2,1)S(1)}, u32[]{:S(2)}, u32[]{:S(2)}) collective-permute-start(bf16[2,32,2048]{2,1,0:T(8,128)(2,1)S(1)} %get-tuple-element.47), channel_id=1, source_target_pairs={{0,2},{1,3},{2,0},{3,1},{4,6},{5,7},{6,4},{7,5},{8,10},{9,11},{10,... | collective-permute-start | bytes 786440 | tf_op jit(solution)/shard_map/ppermute | solution.py:37
  129.2 21.5 %collective-permute-start.3 = (bf16[2,32,2048]{2,1,0:T(8,128)(2,1)S(1)}, bf16[2,32,2048]{2,1,0:T(8,128)(2,1)S(1)}, u32[]{:S(2)}, u32[]{:S(2)}) collective-permute-start(bf16[2,32,2048]{2,1,0:T(8,128)(2,1)S(1)} %get-tuple-element.48), channel_id=1, source_target_pairs={{0,1},{1,0},{2,3},{3,2},{4,5},{5,4},{6,7},{7,6},{8,9},{9,8},{10,11... | collective-permute-start | bytes 786440 | tf_op jit(solution)/shard_map/ppermute | solution.py:37
  159.2 37.8 %all-to-all-start.1 = ((bf16[256,8,256]{0,2,1:T(8,128)(2,1)}), bf16[256,8,256]{0,2,1:T(8,128)(2,1)}, u32[]{:S(2)}, u32[]{:S(2)}) async-start(bf16[256,8,256]{0,2,1:T(8,128)(2,1)} %bitcast.218), calls=%async_computation.1 | async-start | bytes 2097152 | tf_op jit(solution)/shard_map/all_to_all | solution.py:251
  163.4 524.6 %reduce-scatter.8.cloned.1.call-start = ((), (), s32[]{:S(2)}) async-start(), calls=%async_computation.14 | async-start | bytes 9437184 | tf_op jit(solution)/shard_map/reduce_scatter | solution.py:220
  360.0 408.4 %reduce-scatter.6.cloned.1.call-start = ((), (), s32[]{:S(2)}) async-start(), calls=%async_computation.12 | async-start | bytes 9437184 | tf_op jit(solution)/shard_map/reduce_scatter | solution.py:220
  385.9 92.5 %collective-permute-start.12 = (bf16[1024,2048]{1,0:T(8,128)(2,1)}, bf16[1024,2048]{1,0:T(8,128)(2,1)}, u32[]{:S(2)}, u32[]{:S(2)}) collective-permute-start(bf16[1024,2048]{1,0:T(8,128)(2,1)} %reduce-precision_convert_fusion.7), channel_id=1, source_target_pairs={{0,1},{3,2},{4,5},{7,6},{8,9},{11,10},{12,13},{15,14},{16,17},{19,... | collective-permute-start | bytes 12582920 | tf_op jit(solution)/shard_map/ppermute | solution.py:167
  427.4 140.9 %collective-permute-start.15 = (bf16[1024,2048]{1,0:T(8,128)(2,1)}, bf16[1024,2048]{1,0:T(8,128)(2,1)}, u32[]{:S(2)}, u32[]{:S(2)}) collective-permute-start(bf16[1024,2048]{1,0:T(8,128)(2,1)} %reduce-precision_convert_fusion.4), channel_id=1, source_target_pairs={{0,1},{3,2},{4,5},{7,6},{8,9},{11,10},{12,13},{15,14},{16,17},{19,... | collective-permute-start | bytes 12582920 | tf_op jit(solution)/shard_map/ppermute | solution.py:167
  445.3 190.0 %collective-permute-start.6 = (bf16[768,2048]{1,0:T(8,128)(2,1)}, bf16[768,2048]{1,0:T(8,128)(2,1)}, u32[]{:S(2)}, u32[]{:S(2)}) collective-permute-start(bf16[768,2048]{1,0:T(8,128)(2,1)} %reduce-precision_convert_fusion.10), channel_id=1, source_target_pairs={{0,1},{3,2},{4,5},{7,6},{8,9},{11,10},{12,13},{15,14},{16,17},{19,... | collective-permute-start | bytes 9437192 | tf_op jit(solution)/shard_map/ppermute | solution.py:167
  486.2 185.3 %collective-permute-start.13 = (bf16[1024,2048]{1,0:T(8,128)(2,1)}, bf16[1024,2048]{1,0:T(8,128)(2,1)}, u32[]{:S(2)}, u32[]{:S(2)}) collective-permute-start(bf16[1024,2048]{1,0:T(8,128)(2,1)} %reduce-precision_convert_fusion.6), channel_id=1, source_target_pairs={{1,2},{2,1},{5,6},{6,5},{9,10},{10,9},{13,14},{14,13},{17,18},{18,... | collective-permute-start | bytes 12582920 | tf_op jit(solution)/shard_map/ppermute | solution.py:169
  492.6 151.3 %all-to-all-start.7 = ((bf16[8,256,256]{2,1,0:T(8,128)(2,1)}), bf16[8,256,256]{2,1,0:T(8,128)(2,1)S(1)}, u32[]{:S(2)}, u32[]{:S(2)}) async-start(bf16[8,256,256]{2,1,0:T(8,128)(2,1)} %bitcast.77), calls=%async_computation.9 | async-start | bytes 2097152 | tf_op jit(solution)/shard_map/all_to_all | solution.py:299
  576.0 179.4 %collective-permute-start.16 = (bf16[1024,2048]{1,0:T(8,128)(2,1)}, bf16[1024,2048]{1,0:T(8,128)(2,1)}, u32[]{:S(2)}, u32[]{:S(2)}) collective-permute-start(bf16[1024,2048]{1,0:T(8,128)(2,1)} %reduce-precision_convert_fusion.3), channel_id=1, source_target_pairs={{1,2},{2,1},{5,6},{6,5},{9,10},{10,9},{13,14},{14,13},{17,18},{18,... | collective-permute-start | bytes 12582920 | tf_op jit(solution)/shard_map/ppermute | solution.py:169
  641.4 39.2 %collective-permute-start.7 = (bf16[768,2048]{1,0:T(8,128)(2,1)}, bf16[768,2048]{1,0:T(8,128)(2,1)}, u32[]{:S(2)}, u32[]{:S(2)}) collective-permute-start(bf16[768,2048]{1,0:T(8,128)(2,1)} %reduce-precision_convert_fusion.9), channel_id=1, source_target_pairs={{1,2},{2,1},{5,6},{6,5},{9,10},{10,9},{13,14},{14,13},{17,18},{18,... | collective-permute-start | bytes 9437192 | tf_op jit(solution)/shard_map/ppermute | solution.py:169
  644.1 26.3 %collective-permute-start.9 = (bf16[256,2048]{1,0:T(8,128)(2,1)S(1)}, bf16[256,2048]{1,0:T(8,128)(2,1)S(1)}, u32[]{:S(2)}, u32[]{:S(2)}) collective-permute-start(bf16[256,2048]{1,0:T(8,128)(2,1)S(1)} %bitcast.212), channel_id=1, source_target_pairs={{0,1},{3,2},{4,5},{7,6},{8,9},{11,10},{12,13},{15,14},{16,17},{19,... | collective-permute-start | bytes 3145736 | tf_op jit(solution)/shard_map/ppermute | solution.py:167
  670.8 93.5 %collective-permute-start.10 = (bf16[256,2048]{1,0:T(8,128)(2,1)S(1)}, bf16[256,2048]{1,0:T(8,128)(2,1)S(1)}, u32[]{:S(2)}, u32[]{:S(2)}) collective-permute-start(bf16[256,2048]{1,0:T(8,128)(2,1)S(1)} %reduce-precision_convert_fusion.12), channel_id=1, source_target_pairs={{1,2},{2,1},{5,6},{6,5},{9,10},{10,9},{13,14},{14,13},{17,18},{18,... | collective-permute-start | bytes 3145736 | tf_op jit(solution)/shard_map/ppermute | solution.py:169
  679.3 334.9 %collective-permute-start.14 = (bf16[1024,2048]{1,0:T(8,128)(2,1)}, bf16[1024,2048]{1,0:T(8,128)(2,1)}, u32[]{:S(2)}, u32[]{:S(2)}) collective-permute-start(bf16[1024,2048]{1,0:T(8,128)(2,1)} %reduce-precision_convert_fusion.5), channel_id=1, source_target_pairs={{1,0},{2,3},{5,4},{6,7},{9,8},{10,11},{13,12},{14,15},{17,16},{18,... | collective-permute-start | bytes 12582920 | tf_op jit(solution)/shard_map/ppermute | solution.py:171
  686.7 322.5 %collective-permute-start.8 = (bf16[768,2048]{1,0:T(8,128)(2,1)}, bf16[768,2048]{1,0:T(8,128)(2,1)}, u32[]{:S(2)}, u32[]{:S(2)}) collective-permute-start(bf16[768,2048]{1,0:T(8,128)(2,1)} %reduce-precision_convert_fusion.8), channel_id=1, source_target_pairs={{1,0},{2,3},{5,4},{6,7},{9,8},{10,11},{13,12},{14,15},{17,16},{18,... | collective-permute-start | bytes 9437192 | tf_op jit(solution)/shard_map/ppermute | solution.py:171
  691.3 170.7 %all-to-all-start.5 = ((bf16[2,128,2048]{2,0,1:T(2,128)(2,1)}), bf16[2,128,2048]{2,0,1:T(2,128)(2,1)}, u32[]{:S(2)}, u32[]{:S(2)}) async-start(bf16[2,128,2048]{2,0,1:T(2,128)(2,1)} %copy.195), calls=%async_computation.7 | async-start | bytes 2097152 | tf_op jit(solution)/shard_map/all_to_all | solution.py:221
  755.3 116.7 %reduce-scatter.10.cloned.1.call-start = ((), (), s32[]{:S(2)}) async-start(), calls=%async_computation.15 | async-start | bytes 1179648
  763.0 265.8 %collective-permute-start.17 = (bf16[1024,2048]{1,0:T(8,128)(2,1)}, bf16[1024,2048]{1,0:T(8,128)(2,1)}, u32[]{:S(2)}, u32[]{:S(2)}) collective-permute-start(bf16[1024,2048]{1,0:T(8,128)(2,1)} %reduce-precision_convert_fusion.2), channel_id=1, source_target_pairs={{1,0},{2,3},{5,4},{6,7},{9,8},{10,11},{13,12},{14,15},{17,16},{18,... | collective-permute-start | bytes 12582920 | tf_op jit(solution)/shard_map/ppermute | solution.py:171
  765.7 234.6 %collective-permute-start.11 = (bf16[256,2048]{1,0:T(8,128)(2,1)}, bf16[256,2048]{1,0:T(8,128)(2,1)}, u32[]{:S(2)}, u32[]{:S(2)}) collective-permute-start(bf16[256,2048]{1,0:T(8,128)(2,1)} %reduce-precision_convert_fusion.11), channel_id=1, source_target_pairs={{1,0},{2,3},{5,4},{6,7},{9,8},{10,11},{13,12},{14,15},{17,16},{18,... | collective-permute-start | bytes 3145736 | tf_op jit(solution)/shard_map/ppermute | solution.py:171
  768.4 102.9 %copy-start.4 = (bf16[2,4,8,32,768]{4,3,2,1,0:T(8,128)(2,1)S(1)}, bf16[2,4,8,32,768]{4,3,2,1,0:T(8,128)(2,1)}, u32[]{:S(2)}) copy-start(bf16[2,4,8,32,768]{4,3,2,1,0:T(8,128)(2,1)} %concatenate.117) | copy-start | bytes 9437188
  862.1 143.6 %all-to-all-start.2 = ((bf16[2,128,2048]{2,0,1:T(2,128)(2,1)}), bf16[2,128,2048]{2,0,1:T(2,128)(2,1)}, u32[]{:S(2)}, u32[]{:S(2)}) async-start(bf16[2,128,2048]{2,0,1:T(2,128)(2,1)} %copy.179), calls=%async_computation.3 | async-start | bytes 2097152 | tf_op jit(solution)/shard_map/all_to_all | solution.py:221
  1005.6 18.9 %all-to-all-start.6 = ((bf16[8,32,2048]{2,1,0:T(8,128)(2,1)}), bf16[8,32,2048]{2,1,0:T(8,128)(2,1)S(1)}, u32[]{:S(2)}, u32[]{:S(2)}) async-start(bf16[8,32,2048]{2,1,0:T(8,128)(2,1)} %bitcast.66), calls=%async_computation.8 | async-start | bytes 2097152 | tf_op jit(solution)/shard_map/all_to_all | solution.py:222
  1024.6 19.7 %all-to-all-start.3 = ((bf16[8,32,2048]{2,1,0:T(8,128)(2,1)}), bf16[8,32,2048]{2,1,0:T(8,128)(2,1)}, u32[]{:S(2)}, u32[]{:S(2)}) async-start(bf16[8,32,2048]{2,1,0:T(8,128)(2,1)} %bitcast.33), calls=%async_computation.4 | async-start | bytes 2097152 | tf_op jit(solution)/shard_map/all_to_all | solution.py:222
  (44 other events, 572.0 us)
Sparse Core Ops, SparseCore 0:
  82.2 60.9 all-gather.3
  157.0 63.3 all-gather.5
  360.2 69.6 reduce-scatter.7
  434.2 78.6 reduce-scatter.5
  768.5 44.9 reduce-scatter.9
